TPU v7x, 512 devices: a whole 4x8x8 slice. The times are simulated.
512 devices in a mesh: seq: 16 (over y_hi, z), head: 32 (over x, y_lo, core).
Axes of the slice: x: 4, y: 8 (y_hi: 2, y_lo: 4; y = y_hi * 4 + y_lo), z: 8, core: 2. Of those that a mesh axis runs over, the one named last changes fastest.
Arguments:
- tokens: bfloat16 [16384, 4096], P(('seq', 'head')), may hold values from -6 to 6
- doc_lengths: int32 [16], replicated, may hold values from 1 to 8704, as said below
- value_weight: bfloat16 [4096, 8192], P('seq', 'head'), may hold values from -0.09375 to 0.09375
- gate_weight: bfloat16 [4096, 8192], P('seq', 'head'), may hold values from -0.09375 to 0.09375
- state_weight: bfloat16 [8, 4096, 256], P(None, 'seq'), may hold values from -0.09375 to 0.09375
- step_weight: bfloat16 [4096, 128], P('seq', 'head'), may hold values from -0.09375 to 0.09375
- value_conv: float32 [4, 8192], P(None, 'head'), may hold values from -3 to 3
- state_conv: float32 [8, 4, 256], replicated, may hold values from -3 to 3
- step_bias: float32 [128], P('head'), may hold values from -5 to -3
- log_rate: float32 [128], P('head'), may hold values from -6 to 4
Outputs:
- layer_output: bfloat16 [16384, 8192], P('seq', 'head')
Inputs may be any that keep to these rules, and one draw needn't show every extreme that they name: `doc_lengths`: the 16 documents lie one after another, their lengths sum to 16384, and the last one holds 8704 positions.
All inputs are finite; a program needn't handle non-finite values.
Results may differ from a plain program's by a relative error of at most 0.015.
Values may be sent and summed in bfloat16 or wider, within the bound.
No kernel may reach another device: no remote copies, remote signals or barrier semaphores. Data moves between devices by JAX's collectives and lax.ppermute only.
A program may use at most 64 MiB of HBM per device.

v0:
```python
import jax
import jax.numpy as jnp
from jax import lax
from jax.sharding import PartitionSpec as P

HEADS = 128
GROUPS = 8
BLOCK = 256


def passed_along(value, axis, steps):
    count = lax.axis_size(axis)
    leading, last = (max(0, -steps), min(count, count - steps))
    return lax.ppermute(value, axis, [(source, source + steps) for source in range(leading, last)])


def segment_of(positions, starts):
    reached = (starts[None, :] <= positions[:, None]).astype(jnp.int32)
    return jnp.sum(reached, axis=1) - 1


def causal_conv(extended, taps_weight, seg_ext, row_count):
    tap_count = taps_weight.shape[0]
    own_segment = seg_ext[tap_count - 1 :]
    summed = jnp.zeros((row_count, extended.shape[1]), jnp.float32)
    for tap_index in range(tap_count):
        window = extended[tap_index : tap_index + row_count].astype(jnp.float32)
        keep_mask = (seg_ext[tap_index : tap_index + row_count] == own_segment).astype(jnp.float32)[
            :, None
        ]
        summed = summed + taps_weight[tap_index][None, :] * window * keep_mask
    return jax.nn.silu(summed).astype(jnp.bfloat16)


def block_terms(b_rows, c_rows, x_rows, decay_rows, step_rows, segments, seg_before):
    block_len = b_rows.shape[0]
    head_total = decay_rows.shape[0]
    x_heads = x_rows.reshape(block_len, head_total, -1)
    cumulative = jnp.cumsum(decay_rows, axis=1)
    products = jnp.dot(c_rows, b_rows.T, preferred_element_type=jnp.float32)
    local_index = jnp.arange(block_len)
    allowed = (local_index[None, :] <= local_index[:, None]) & (
        segments[None, :] == segments[:, None]
    )
    spread = cumulative[:, :, None] - cumulative[:, None, :]
    decay_mat = jnp.where(allowed[None], jnp.exp(jnp.where(allowed[None], spread, 0.0)), 0.0)
    scores = (products[None] * decay_mat * step_rows[:, None, :]).astype(jnp.bfloat16)
    y_inner = jnp.einsum("hij,jhp->ihp", scores, x_heads, preferred_element_type=jnp.float32)
    ending = cumulative[:, -1]
    trailing = (
        jnp.where((segments == segments[-1])[None, :], jnp.exp(ending[:, None] - cumulative), 0.0)
        * step_rows
    )
    weighted = (trailing.T[:, :, None] * x_heads.astype(jnp.float32)).astype(jnp.bfloat16)
    local_state = jnp.einsum("jn,jhp->hnp", b_rows, weighted, preferred_element_type=jnp.float32)
    factor = jnp.where(segments[-1] == seg_before, jnp.exp(ending), 0.0)
    entry_gain = jnp.where((segments == seg_before)[None, :], jnp.exp(cumulative), 0.0)
    return (y_inner.reshape(block_len, -1), local_state, factor, entry_gain)


def local_pass(state_cols, value_cols, decay_cols, step_cols, seg_rows, seg_before, block_len):
    block_count = state_cols.shape[0] // block_len
    state_dim = state_cols.shape[1] // 2
    head_total = decay_cols.shape[1]
    b_all = state_cols[:, :state_dim].reshape(block_count, block_len, state_dim)
    c_all = state_cols[:, state_dim:].reshape(block_count, block_len, state_dim)
    x_all = value_cols.reshape(block_count, block_len, -1)
    decay_all = decay_cols.reshape(block_count, block_len, head_total).transpose(0, 2, 1)
    step_all = step_cols.reshape(block_count, block_len, head_total).transpose(0, 2, 1)
    seg_all = seg_rows.reshape(block_count, block_len)

    def one_block(block_item):
        return block_terms(*block_item)

    outputs = lax.map(one_block, (b_all, c_all, x_all, decay_all, step_all, seg_all, seg_before))
    return (outputs, c_all)


def prefix_blocks(local_state, factor):

    def chain_step(carry_pair, block_item):
        running, running_gain = carry_pair
        local_term, factor_term = block_item
        return (
            (factor_term[:, None, None] * running + local_term, factor_term * running_gain),
            (running, running_gain),
        )

    initial = (
        jnp.zeros(local_state.shape[1:], jnp.float32),
        jnp.ones((factor.shape[1],), jnp.float32),
    )
    (shard_state, shard_gain), (inside, gain_list) = lax.scan(
        chain_step, initial, (local_state, factor)
    )
    return (shard_state, shard_gain, inside, gain_list)


def finish(y_inner, incoming, entry_gain, c_all, value_cols, gate_cols):
    block_count, block_len, _ = y_inner.shape
    head_total = incoming.shape[1]
    carried = jnp.einsum(
        "cin,chnp->cihp", c_all.astype(jnp.float32), incoming, precision=lax.Precision.HIGHEST
    )
    carried = carried * entry_gain.transpose(0, 2, 1)[:, :, :, None]
    x_heads = value_cols.reshape(block_count, block_len, head_total, -1).astype(jnp.float32)
    summed = y_inner.reshape(block_count, block_len, head_total, -1) + carried + x_heads
    gating = jax.nn.silu(gate_cols.astype(jnp.float32)).reshape(
        block_count, block_len, head_total, -1
    )
    return (summed * gating).reshape(block_count * block_len, -1).astype(jnp.bfloat16)


def local(
    tokens,
    doc_lengths,
    value_weight,
    gate_weight,
    state_weight,
    step_weight,
    value_conv,
    state_conv,
    step_bias,
    log_rate,
):
    tok_dev = tokens.shape[0] * lax.axis_size("head")
    heads_here = step_weight.shape[1]
    tap_count = value_conv.shape[0]
    group_index = lax.axis_index("head") * heads_here // (HEADS // GROUPS)
    state_own = lax.dynamic_index_in_dim(state_weight, group_index, 0, keepdims=False)
    conv_own = lax.dynamic_index_in_dim(state_conv, group_index, 0, keepdims=False)
    gathered = lax.all_gather(tokens, "head", axis=0, tiled=True)
    shard_pieces = (
        lax.all_gather(value_weight, "seq", axis=0, tiled=True),
        lax.all_gather(gate_weight, "seq", axis=0, tiled=True),
        lax.all_gather(state_own, "seq", axis=0, tiled=True),
        lax.all_gather(step_weight, "seq", axis=0, tiled=True),
    )
    projected = tuple(
        (
            jnp.dot(gathered, weight_piece, preferred_element_type=jnp.float32)
            for weight_piece in shard_pieces
        )
    )
    value_proj = projected[0].astype(jnp.bfloat16)
    gate_proj = projected[1].astype(jnp.bfloat16)
    state_proj = projected[2].astype(jnp.bfloat16)
    step_proj = projected[3].astype(jnp.bfloat16)
    value_cols = value_proj.shape[1]
    rim_source = jnp.concatenate(
        [value_proj[-(tap_count - 1) :], state_proj[-(tap_count - 1) :]], axis=1
    )
    rim_rows = passed_along(rim_source, "seq", 1)
    value_ext = jnp.concatenate([rim_rows[:, :value_cols], value_proj], axis=0)
    state_ext = jnp.concatenate([rim_rows[:, value_cols:], state_proj], axis=0)
    starts = jnp.cumsum(doc_lengths) - doc_lengths
    positions = lax.axis_index("seq") * tok_dev + jnp.arange(-(tap_count - 1), tok_dev)
    seg_ext = segment_of(positions, starts)
    value_act = causal_conv(value_ext, value_conv, seg_ext, tok_dev)
    state_act = causal_conv(state_ext, conv_own, seg_ext, tok_dev)
    step_size = jax.nn.softplus(step_proj.astype(jnp.float32) + step_bias[None, :])
    decay_rate = -jnp.exp(log_rate)[None, :] * step_size
    seg_rows = seg_ext[tap_count - 1 :]
    seg_before = seg_ext[tap_count - 2 : tap_count - 2 + tok_dev : BLOCK]
    (y_inner, local_state, factor, entry_gain), c_all = local_pass(
        state_act, value_act, decay_rate, step_size, seg_rows, seg_before, BLOCK
    )
    shard_state, shard_gain, inside, gain_list = prefix_blocks(local_state, factor)

    def relay(step_index, arriving):
        leaving = shard_gain[:, None, None] * arriving + shard_state
        return passed_along(leaving, "seq", 1)

    entering = lax.fori_loop(0, lax.axis_size("seq") - 1, relay, jnp.zeros_like(shard_state))
    incoming = inside + gain_list[:, :, None, None] * entering[None]
    return finish(y_inner, incoming, entry_gain, c_all, value_act, gate_proj)


def solution(mesh):
    return jax.shard_map(
        local,
        mesh=mesh,
        in_specs=(
            P(("seq", "head"), None),
            P(),
            P("seq", "head"),
            P("seq", "head"),
            P(None, "seq", None),
            P("seq", "head"),
            P(None, "head"),
            P(),
            P("head"),
            P("head"),
        ),
        out_specs=P("seq", "head"),
        check_vma=False,
    )
```

profile of v0, /device:TPU:48, one launch (start us, length us, event | category | flops | bytes accessed | tf_op | source)
XLA Modules:
  0.0 720.9 jit_solution(3404737921538199455)
XLA Ops:
  11.2 56.0 %all_gather.18 = bf16[4096,4]{0,1:T(4,128)(2,1)S(1)} all-gather(bf16[256,4]{0,1:T(4,128)(2,1)} %param.21), channel_id=1, replica_groups=mesh['seq'=16,'head'=32] {'seq'}, dimensions={0}, use_global_device_ids=true | all-gather | bytes 34816 | tf_op jit(solution)/shard_map/all_gather | solution.py:137
  69.7 48.0 %all-gather.8.cloned.1.call-done = bf16[4096,256]{1,0:T(8,128)(2,1)} async-done(((bf16[256,256]{1,0:T(8,128)(2,1)}), bf16[4096,256]{1,0:T(8,128)(2,1)}) %all-gather.8.cloned.1.call-update) | async-done | bytes 2097168 | tf_op jit(solution)/shard_map/all_gather | solution.py:134
  117.7 69.9 %all-gather.6.cloned.1.call-done = bf16[1024,4096]{1,0:T(8,128)(2,1)} async-done(((bf16[32,4096]{1,0:T(8,128)(2,1)}), bf16[1024,4096]{1,0:T(8,128)(2,1)}) %all-gather.6.cloned.1.call-update) | async-done | bytes 8388624 | tf_op jit(solution)/shard_map/all_gather | solution.py:132
  187.6 6.3 convolution_convert_fusion.1
  194.7 98.4 %all-gather.12.cloned.1.call-done = bf16[1,4096,256]{2,1,0:T(8,128)(2,1)} async-done(((bf16[1,256,256]{2,1,0:T(8,128)(2,1)}), bf16[1,4096,256]{2,1,0:T(8,128)(2,1)}) %all-gather.12.cloned.1.call-update) | async-done | bytes 2097168 | tf_op jit(solution)/shard_map/all_gather | solution.py:136
  293.1 6.3 fusion.29
  300.3 3.0 collective-permute-start.1
  303.3 92.2 %all-gather.10.cloned.1.call-done = bf16[4096,256]{1,0:T(8,128)(2,1)} async-done(((bf16[256,256]{1,0:T(8,128)(2,1)}), bf16[4096,256]{1,0:T(8,128)(2,1)}) %all-gather.10.cloned.1.call-update) | async-done | bytes 2097168 | tf_op jit(solution)/shard_map/all_gather | solution.py:135
  395.5 7.4 %convert_multiply_fusion = f32[1024,256]{1,0:T(8,128)} fusion(bf16[1024,4096]{1,0:T(8,128)(2,1)} %all-gather.6.cloned.1.call-done, bf16[4096,256]{1,0:T(8,128)(2,1)} %all-gather.10.cloned.1.call-done), kind=kOutput, calls=%fused_computation.49 | convolution fusion | flops 2149056512 | bytes 11534336 | tf_op jit(solution)/shard_map/dot_general | solution.py:141
  402.9 5.7 broadcast_multiply_fusion
  408.6 2.1 reshape.258
  412.3 2.7 multiply_convert_fusion.3
  416.1 2.2 reshape.257
  418.4 30.8 %while.43 = (s32[]{:T(128)}, f32[4,256,256]{1,2,0:T(8,128)}, f32[4,4,128,64]{2,3,1,0:T(8,128)S(1)}, f32[4,4]{1,0:T(4,128)S(1)}, f32[4,4,256]{2,1,0:T(4,128)S(1)}...) while((s32[]{:T(128)}, f32[4,256,256]{1,2,0:T(8,128)}, ...), condition=%wide.region_5.6_spmd, body=%wide.region_2.5_spmd.sunk | while | flops 69210640 | bytes 2915319 | solution.py:75
  449.9 4.2 while.45
  454.1 247.6 %while.44 = (s32[]{:T(128)}, f32[4,128,64]{2,1,0:T(8,128)S(1)}, f32[4]{0:T(128)S(1)}, f32[4,128,64]{2,1,0:T(8,128)S(1)}, s32[]{:T(128)}) while((s32[]{:T(128)}, f32[4,128,64]{2,1,0:T(8,128)S(1)}, f32[4]{0:T(128)S(1)}, f32[4,128,64]{2,1,0:T(8,128)S(1)}, s32[]{:T(128)}) %tuple.85), condition=%wide.region_9.10_spmd, body=%wide.region_8.9_spmd.sunk | while | flops 65538 | bytes 917621 | solution.py:174
  454.2 3.0 collective-permute-start
  457.2 12.6 %collective-permute-done = f32[4,128,64]{2,1,0:T(8,128)S(1)} collective-permute-done((f32[4,128,64]{2,1,0:T(8,128)S(1)}, f32[4,128,64]{2,1,0:T(8,128)S(1)}, u32[]{:S(2)}, u32[]{:S(2)}) %collective-permute-start) | collective-permute-done | bytes 131104 | tf_op jit(solution)/shard_map/while/body/eval_jaxpr/ppermute | solution.py:14
  469.9 1.9 collective-permute-start
  471.8 15.3 %collective-permute-done = f32[4,128,64]{2,1,0:T(8,128)S(1)} collective-permute-done((f32[4,128,64]{2,1,0:T(8,128)S(1)}, f32[4,128,64]{2,1,0:T(8,128)S(1)}, u32[]{:S(2)}, u32[]{:S(2)}) %collective-permute-start) | collective-permute-done | bytes 131104 | tf_op jit(solution)/shard_map/while/body/eval_jaxpr/ppermute | solution.py:14
  487.2 1.9 collective-permute-start
  489.1 15.1 %collective-permute-done = f32[4,128,64]{2,1,0:T(8,128)S(1)} collective-permute-done((f32[4,128,64]{2,1,0:T(8,128)S(1)}, f32[4,128,64]{2,1,0:T(8,128)S(1)}, u32[]{:S(2)}, u32[]{:S(2)}) %collective-permute-start) | collective-permute-done | bytes 131104 | tf_op jit(solution)/shard_map/while/body/eval_jaxpr/ppermute | solution.py:14
  504.3 1.9 collective-permute-start
  506.2 15.1 %collective-permute-done = f32[4,128,64]{2,1,0:T(8,128)S(1)} collective-permute-done((f32[4,128,64]{2,1,0:T(8,128)S(1)}, f32[4,128,64]{2,1,0:T(8,128)S(1)}, u32[]{:S(2)}, u32[]{:S(2)}) %collective-permute-start) | collective-permute-done | bytes 131104 | tf_op jit(solution)/shard_map/while/body/eval_jaxpr/ppermute | solution.py:14
  521.4 1.9 collective-permute-start
  523.3 19.9 %collective-permute-done = f32[4,128,64]{2,1,0:T(8,128)S(1)} collective-permute-done((f32[4,128,64]{2,1,0:T(8,128)S(1)}, f32[4,128,64]{2,1,0:T(8,128)S(1)}, u32[]{:S(2)}, u32[]{:S(2)}) %collective-permute-start) | collective-permute-done | bytes 131104 | tf_op jit(solution)/shard_map/while/body/eval_jaxpr/ppermute | solution.py:14
  543.3 1.9 collective-permute-start
  545.2 17.7 %collective-permute-done = f32[4,128,64]{2,1,0:T(8,128)S(1)} collective-permute-done((f32[4,128,64]{2,1,0:T(8,128)S(1)}, f32[4,128,64]{2,1,0:T(8,128)S(1)}, u32[]{:S(2)}, u32[]{:S(2)}) %collective-permute-start) | collective-permute-done | bytes 131104 | tf_op jit(solution)/shard_map/while/body/eval_jaxpr/ppermute | solution.py:14
  563.0 1.9 collective-permute-start
  564.9 15.2 %collective-permute-done = f32[4,128,64]{2,1,0:T(8,128)S(1)} collective-permute-done((f32[4,128,64]{2,1,0:T(8,128)S(1)}, f32[4,128,64]{2,1,0:T(8,128)S(1)}, u32[]{:S(2)}, u32[]{:S(2)}) %collective-permute-start) | collective-permute-done | bytes 131104 | tf_op jit(solution)/shard_map/while/body/eval_jaxpr/ppermute | solution.py:14
  580.2 1.9 collective-permute-start
  582.1 14.3 %collective-permute-done = f32[4,128,64]{2,1,0:T(8,128)S(1)} collective-permute-done((f32[4,128,64]{2,1,0:T(8,128)S(1)}, f32[4,128,64]{2,1,0:T(8,128)S(1)}, u32[]{:S(2)}, u32[]{:S(2)}) %collective-permute-start) | collective-permute-done | bytes 131104 | tf_op jit(solution)/shard_map/while/body/eval_jaxpr/ppermute | solution.py:14
  596.5 1.9 collective-permute-start
  598.4 16.3 %collective-permute-done = f32[4,128,64]{2,1,0:T(8,128)S(1)} collective-permute-done((f32[4,128,64]{2,1,0:T(8,128)S(1)}, f32[4,128,64]{2,1,0:T(8,128)S(1)}, u32[]{:S(2)}, u32[]{:S(2)}) %collective-permute-start) | collective-permute-done | bytes 131104 | tf_op jit(solution)/shard_map/while/body/eval_jaxpr/ppermute | solution.py:14
  614.8 1.9 collective-permute-start
  616.8 13.1 %collective-permute-done = f32[4,128,64]{2,1,0:T(8,128)S(1)} collective-permute-done((f32[4,128,64]{2,1,0:T(8,128)S(1)}, f32[4,128,64]{2,1,0:T(8,128)S(1)}, u32[]{:S(2)}, u32[]{:S(2)}) %collective-permute-start) | collective-permute-done | bytes 131104 | tf_op jit(solution)/shard_map/while/body/eval_jaxpr/ppermute | solution.py:14
  629.9 1.9 collective-permute-start
  631.9 12.4 %collective-permute-done = f32[4,128,64]{2,1,0:T(8,128)S(1)} collective-permute-done((f32[4,128,64]{2,1,0:T(8,128)S(1)}, f32[4,128,64]{2,1,0:T(8,128)S(1)}, u32[]{:S(2)}, u32[]{:S(2)}) %collective-permute-start) | collective-permute-done | bytes 131104 | tf_op jit(solution)/shard_map/while/body/eval_jaxpr/ppermute | solution.py:14
  644.3 1.9 collective-permute-start
  646.3 12.4 %collective-permute-done = f32[4,128,64]{2,1,0:T(8,128)S(1)} collective-permute-done((f32[4,128,64]{2,1,0:T(8,128)S(1)}, f32[4,128,64]{2,1,0:T(8,128)S(1)}, u32[]{:S(2)}, u32[]{:S(2)}) %collective-permute-start) | collective-permute-done | bytes 131104 | tf_op jit(solution)/shard_map/while/body/eval_jaxpr/ppermute | solution.py:14
  658.7 1.9 collective-permute-start
  660.6 12.4 %collective-permute-done = f32[4,128,64]{2,1,0:T(8,128)S(1)} collective-permute-done((f32[4,128,64]{2,1,0:T(8,128)S(1)}, f32[4,128,64]{2,1,0:T(8,128)S(1)}, u32[]{:S(2)}, u32[]{:S(2)}) %collective-permute-start) | collective-permute-done | bytes 131104 | tf_op jit(solution)/shard_map/while/body/eval_jaxpr/ppermute | solution.py:14
  673.1 1.9 collective-permute-start
  675.0 12.4 %collective-permute-done = f32[4,128,64]{2,1,0:T(8,128)S(1)} collective-permute-done((f32[4,128,64]{2,1,0:T(8,128)S(1)}, f32[4,128,64]{2,1,0:T(8,128)S(1)}, u32[]{:S(2)}, u32[]{:S(2)}) %collective-permute-start) | collective-permute-done | bytes 131104 | tf_op jit(solution)/shard_map/while/body/eval_jaxpr/ppermute | solution.py:14
  689.4 12.4 %collective-permute-done = f32[4,128,64]{2,1,0:T(8,128)S(1)} collective-permute-done((f32[4,128,64]{2,1,0:T(8,128)S(1)}, f32[4,128,64]{2,1,0:T(8,128)S(1)}, u32[]{:S(2)}, u32[]{:S(2)}) %collective-permute-start) | collective-permute-done | bytes 131104 | tf_op jit(solution)/shard_map/while/body/eval_jaxpr/ppermute | solution.py:14
  702.9 2.5 copy.51
  705.4 2.6 fusion.48
  709.7 2.6 multiply_convert_fusion.2
  (216 shorter events, 49.8 us)
Async XLA Ops:
  6.5 1.5 copy-start
  6.5 111.1 %all-gather.8.cloned.1.call-start = ((), (), s32[]{:S(2)}) async-start(), calls=%async_computation.1 | async-start | bytes 2228224 | tf_op jit(solution)/shard_map/all_gather | solution.py:134
  7.3 180.3 %all-gather.6.cloned.1.call-start = ((), (), s32[]{:S(2)}) async-start(), calls=%async_computation | async-start | bytes 8650752 | tf_op jit(solution)/shard_map/all_gather | solution.py:132
  8.0 285.1 %all-gather.12.cloned.1.call-start = ((), (), s32[]{:S(2)}) async-start(), calls=%async_computation.3 | async-start | bytes 2228224 | tf_op jit(solution)/shard_map/all_gather | solution.py:136
  8.8 386.7 %all-gather.10.cloned.1.call-start = ((), (), s32[]{:S(2)}) async-start(), calls=%async_computation.2 | async-start | bytes 2228224 | tf_op jit(solution)/shard_map/all_gather | solution.py:135
  193.9 0.8 copy-start.6
  299.4 0.8 copy-start.8
  300.2 102.6 %copy-start.9 = (f32[4]{0:T(128)S(1)}, f32[4]{0:T(128)}, u32[]{:S(2)}) copy-start(f32[4]{0:T(128)} %param.24) | copy-start | bytes 52
  300.3 112.0 %collective-permute-start.1 = (bf16[3,512]{1,0:T(4,128)(2,1)S(1)}, bf16[3,512]{1,0:T(4,128)(2,1)S(1)}, u32[]{:S(2)}, u32[]{:S(2)}) collective-permute-start(bf16[3,512]{1,0:T(4,128)(2,1)S(1)} %pad_maximum_fusion.2), channel_id=1, source_target_pairs={{0,32},{32,64},{64,96},{96,128},{128,160},{160,192},{192,224},{224... | collective-permute-start | bytes 9224 | tf_op jit(solution)/shard_map/ppermute | solution.py:14
  412.3 2.8 copy-start.7
  415.0 3.4 copy-start.5
  449.2 0.7 copy-start.2
  454.1 247.7 %copy-start.4 = (f32[4,4,128,64]{3,2,1,0:T(8,128)S(1)}, f32[4,4,128,64]{3,2,1,0:T(8,128)}, u32[]{:S(2)}) copy-start(f32[4,4,128,64]{3,2,1,0:T(8,128)} %get-tuple-element.135) | copy-start | bytes 1572868
  454.2 15.5 %collective-permute-start = (f32[4,128,64]{2,1,0:T(8,128)S(1)}, f32[4,128,64]{2,1,0:T(8,128)S(1)}, u32[]{:S(2)}, u32[]{:S(2)}) collective-permute-start(f32[4,128,64]{2,1,0:T(8,128)S(1)} %multiply_add_fusion.3), channel_id=1, source_target_pairs={{0,32},{32,64},{64,96},{96,128},{128,160},{160,192},{192,224},{224... | collective-permute-start | bytes 393224 | tf_op jit(solution)/shard_map/while/body/eval_jaxpr/ppermute | solution.py:14
  469.9 17.2 %collective-permute-start = (f32[4,128,64]{2,1,0:T(8,128)S(1)}, f32[4,128,64]{2,1,0:T(8,128)S(1)}, u32[]{:S(2)}, u32[]{:S(2)}) collective-permute-start(f32[4,128,64]{2,1,0:T(8,128)S(1)} %multiply_add_fusion.3), channel_id=1, source_target_pairs={{0,32},{32,64},{64,96},{96,128},{128,160},{160,192},{192,224},{224... | collective-permute-start | bytes 393224 | tf_op jit(solution)/shard_map/while/body/eval_jaxpr/ppermute | solution.py:14
  487.2 17.0 %collective-permute-start = (f32[4,128,64]{2,1,0:T(8,128)S(1)}, f32[4,128,64]{2,1,0:T(8,128)S(1)}, u32[]{:S(2)}, u32[]{:S(2)}) collective-permute-start(f32[4,128,64]{2,1,0:T(8,128)S(1)} %multiply_add_fusion.3), channel_id=1, source_target_pairs={{0,32},{32,64},{64,96},{96,128},{128,160},{160,192},{192,224},{224... | collective-permute-start | bytes 393224 | tf_op jit(solution)/shard_map/while/body/eval_jaxpr/ppermute | solution.py:14
  504.3 17.0 %collective-permute-start = (f32[4,128,64]{2,1,0:T(8,128)S(1)}, f32[4,128,64]{2,1,0:T(8,128)S(1)}, u32[]{:S(2)}, u32[]{:S(2)}) collective-permute-start(f32[4,128,64]{2,1,0:T(8,128)S(1)} %multiply_add_fusion.3), channel_id=1, source_target_pairs={{0,32},{32,64},{64,96},{96,128},{128,160},{160,192},{192,224},{224... | collective-permute-start | bytes 393224 | tf_op jit(solution)/shard_map/while/body/eval_jaxpr/ppermute | solution.py:14
  521.4 21.8 %collective-permute-start = (f32[4,128,64]{2,1,0:T(8,128)S(1)}, f32[4,128,64]{2,1,0:T(8,128)S(1)}, u32[]{:S(2)}, u32[]{:S(2)}) collective-permute-start(f32[4,128,64]{2,1,0:T(8,128)S(1)} %multiply_add_fusion.3), channel_id=1, source_target_pairs={{0,32},{32,64},{64,96},{96,128},{128,160},{160,192},{192,224},{224... | collective-permute-start | bytes 393224 | tf_op jit(solution)/shard_map/while/body/eval_jaxpr/ppermute | solution.py:14
  543.3 19.6 %collective-permute-start = (f32[4,128,64]{2,1,0:T(8,128)S(1)}, f32[4,128,64]{2,1,0:T(8,128)S(1)}, u32[]{:S(2)}, u32[]{:S(2)}) collective-permute-start(f32[4,128,64]{2,1,0:T(8,128)S(1)} %multiply_add_fusion.3), channel_id=1, source_target_pairs={{0,32},{32,64},{64,96},{96,128},{128,160},{160,192},{192,224},{224... | collective-permute-start | bytes 393224 | tf_op jit(solution)/shard_map/while/body/eval_jaxpr/ppermute | solution.py:14
  563.0 17.1 %collective-permute-start = (f32[4,128,64]{2,1,0:T(8,128)S(1)}, f32[4,128,64]{2,1,0:T(8,128)S(1)}, u32[]{:S(2)}, u32[]{:S(2)}) collective-permute-start(f32[4,128,64]{2,1,0:T(8,128)S(1)} %multiply_add_fusion.3), channel_id=1, source_target_pairs={{0,32},{32,64},{64,96},{96,128},{128,160},{160,192},{192,224},{224... | collective-permute-start | bytes 393224 | tf_op jit(solution)/shard_map/while/body/eval_jaxpr/ppermute | solution.py:14
  580.2 16.2 %collective-permute-start = (f32[4,128,64]{2,1,0:T(8,128)S(1)}, f32[4,128,64]{2,1,0:T(8,128)S(1)}, u32[]{:S(2)}, u32[]{:S(2)}) collective-permute-start(f32[4,128,64]{2,1,0:T(8,128)S(1)} %multiply_add_fusion.3), channel_id=1, source_target_pairs={{0,32},{32,64},{64,96},{96,128},{128,160},{160,192},{192,224},{224... | collective-permute-start | bytes 393224 | tf_op jit(solution)/shard_map/while/body/eval_jaxpr/ppermute | solution.py:14
  596.5 18.2 %collective-permute-start = (f32[4,128,64]{2,1,0:T(8,128)S(1)}, f32[4,128,64]{2,1,0:T(8,128)S(1)}, u32[]{:S(2)}, u32[]{:S(2)}) collective-permute-start(f32[4,128,64]{2,1,0:T(8,128)S(1)} %multiply_add_fusion.3), channel_id=1, source_target_pairs={{0,32},{32,64},{64,96},{96,128},{128,160},{160,192},{192,224},{224... | collective-permute-start | bytes 393224 | tf_op jit(solution)/shard_map/while/body/eval_jaxpr/ppermute | solution.py:14
  614.8 15.0 %collective-permute-start = (f32[4,128,64]{2,1,0:T(8,128)S(1)}, f32[4,128,64]{2,1,0:T(8,128)S(1)}, u32[]{:S(2)}, u32[]{:S(2)}) collective-permute-start(f32[4,128,64]{2,1,0:T(8,128)S(1)} %multiply_add_fusion.3), channel_id=1, source_target_pairs={{0,32},{32,64},{64,96},{96,128},{128,160},{160,192},{192,224},{224... | collective-permute-start | bytes 393224 | tf_op jit(solution)/shard_map/while/body/eval_jaxpr/ppermute | solution.py:14
  629.9 14.3 %collective-permute-start = (f32[4,128,64]{2,1,0:T(8,128)S(1)}, f32[4,128,64]{2,1,0:T(8,128)S(1)}, u32[]{:S(2)}, u32[]{:S(2)}) collective-permute-start(f32[4,128,64]{2,1,0:T(8,128)S(1)} %multiply_add_fusion.3), channel_id=1, source_target_pairs={{0,32},{32,64},{64,96},{96,128},{128,160},{160,192},{192,224},{224... | collective-permute-start | bytes 393224 | tf_op jit(solution)/shard_map/while/body/eval_jaxpr/ppermute | solution.py:14
  644.3 14.3 %collective-permute-start = (f32[4,128,64]{2,1,0:T(8,128)S(1)}, f32[4,128,64]{2,1,0:T(8,128)S(1)}, u32[]{:S(2)}, u32[]{:S(2)}) collective-permute-start(f32[4,128,64]{2,1,0:T(8,128)S(1)} %multiply_add_fusion.3), channel_id=1, source_target_pairs={{0,32},{32,64},{64,96},{96,128},{128,160},{160,192},{192,224},{224... | collective-permute-start | bytes 393224 | tf_op jit(solution)/shard_map/while/body/eval_jaxpr/ppermute | solution.py:14
  658.7 14.3 %collective-permute-start = (f32[4,128,64]{2,1,0:T(8,128)S(1)}, f32[4,128,64]{2,1,0:T(8,128)S(1)}, u32[]{:S(2)}, u32[]{:S(2)}) collective-permute-start(f32[4,128,64]{2,1,0:T(8,128)S(1)} %multiply_add_fusion.3), channel_id=1, source_target_pairs={{0,32},{32,64},{64,96},{96,128},{128,160},{160,192},{192,224},{224... | collective-permute-start | bytes 393224 | tf_op jit(solution)/shard_map/while/body/eval_jaxpr/ppermute | solution.py:14
  673.1 14.3 %collective-permute-start = (f32[4,128,64]{2,1,0:T(8,128)S(1)}, f32[4,128,64]{2,1,0:T(8,128)S(1)}, u32[]{:S(2)}, u32[]{:S(2)}) collective-permute-start(f32[4,128,64]{2,1,0:T(8,128)S(1)} %multiply_add_fusion.3), channel_id=1, source_target_pairs={{0,32},{32,64},{64,96},{96,128},{128,160},{160,192},{192,224},{224... | collective-permute-start | bytes 393224 | tf_op jit(solution)/shard_map/while/body/eval_jaxpr/ppermute | solution.py:14
  687.5 14.3 %collective-permute-start = (f32[4,128,64]{2,1,0:T(8,128)S(1)}, f32[4,128,64]{2,1,0:T(8,128)S(1)}, u32[]{:S(2)}, u32[]{:S(2)}) collective-permute-start(f32[4,128,64]{2,1,0:T(8,128)S(1)} %multiply_add_fusion.3), channel_id=1, source_target_pairs={{0,32},{32,64},{64,96},{96,128},{128,160},{160,192},{192,224},{224... | collective-permute-start | bytes 393224 | tf_op jit(solution)/shard_map/while/body/eval_jaxpr/ppermute | solution.py:14
  701.8 3.7 copy-start.3
  702.9 5.1 copy-start.1
Sparse Core Ops, SparseCore 0:
  10.5 107.0 all-gather.7
  119.8 67.7 all-gather.5
  190.7 102.3 all-gather.11
  296.1 99.3 all-gather.9
where the time goes:
time: 722 us; the launch traced here: 721 us
  waiting for transfers between devices  527 us (73%)
  blocking collectives  56 us (8%)
  starting transfers between devices  33 us (5%)
  matrix products  31.8 us (4%)
  local copies, waits for them, and re-layouts  28.9 us (4%)
  other arithmetic  25.4 us (4%)
  between operations  13.3 us (2%)
    ppermute x16, waiting for transfers between devices, passed_along(): lax.ppermute(value, axis, [(source, source + steps) for source in range(l...  216 us
    all_gather x1, waiting for transfers between devices, local(): lax.all_gather(state_own, 'seq', axis=0, tiled=True)  98.4 us
    all_gather x1, waiting for transfers between devices, local(): lax.all_gather(gate_weight, 'seq', axis=0, tiled=True)  92.2 us
    all_gather x1, waiting for transfers between devices, local(): gathered = lax.all_gather(tokens, 'head', axis=0, tiled=True)  69.9 us
    all_gather x1, blocking collectives, local(): lax.all_gather(step_weight, 'seq', axis=0, tiled=True)  56 us
    all_gather x1, waiting for transfers between devices, local(): lax.all_gather(value_weight, 'seq', axis=0, tiled=True)  48 us
    ppermute x16, starting transfers between devices, passed_along(): lax.ppermute(value, axis, [(source, source + steps) for source in range(l...  32.9 us
    dot_general x4, matrix products, local(): jnp.dot(gathered, weight_piece, preferred_element_type=jnp.float32)  25.7 us
  transfers between devices with their start and end apart: 20, of which 19 were waited for; matrix products, arithmetic and copies ran while one was open for 5% of the time, Pallas kernels for 0%

commit v1 on v0

--- a/solution.py
+++ b/solution.py
@@ -6,6 +6,11 @@
 HEADS = 128
 GROUPS = 8
 BLOCK = 256
+
+
+def swapped_in(block, axis, dim):
+    stack = jnp.stack([block] * lax.axis_size(axis))
+    return jnp.concatenate(lax.all_to_all(stack, axis, 0, 0), axis=dim)
 
 
 def passed_along(value, axis, steps):
@@ -129,7 +134,7 @@
     group_index = lax.axis_index("head") * heads_here // (HEADS // GROUPS)
     state_own = lax.dynamic_index_in_dim(state_weight, group_index, 0, keepdims=False)
     conv_own = lax.dynamic_index_in_dim(state_conv, group_index, 0, keepdims=False)
-    gathered = lax.all_gather(tokens, "head", axis=0, tiled=True)
+    gathered = swapped_in(tokens, "head", 0)
     shard_pieces = (
         lax.all_gather(value_weight, "seq", axis=0, tiled=True),
         lax.all_gather(gate_weight, "seq", axis=0, tiled=True),

time: 722 us -> 700 us (0.970)
  waiting for transfers between devices: 527 us -> 384 us
  blocking collectives: 56 us -> 160 us
  local copies, waits for them, and re-layouts: 28.9 us -> 37.9 us
    all_gather x1, blocking collectives: 56 us -> 160 us  [local(): lax.all_gather(step_weight, 'seq', axis=0, tiled=True)]
    all_gather x1, waiting for transfers between devices: 98.4 us -> 0.01 us  [local(): lax.all_gather(state_own, 'seq', axis=0, tiled=True)]
    all_gather x1 -> x0, waiting for transfers between devices: 69.9 us -> none  [local(): gathered = lax.all_gather(tokens, 'head', axis=0, tiled=True)]
    all_to_all x0 -> x1, waiting for transfers between devices: none -> 68.6 us  [swapped_in(): return jnp.concatenate(lax.all_to_all(stack, axis, 0, 0), axis=dim)]
    all_gather x1, waiting for transfers between devices: 48 us -> 4.51 us  [local(): lax.all_gather(value_weight, 'seq', axis=0, tiled=True)]
  transfers between devices with their start and end apart: 20 -> 20, of which waited for: 19 -> 18; matrix products, arithmetic and copies ran while one was open for 5% -> 4% of each run, Pallas kernels for 0% -> 0%
where the time goes in v1:
time: 700 us; the launch traced here: 699 us
  waiting for transfers between devices  384 us (55%)
  blocking collectives  160 us (23%)
  starting transfers between devices  39.1 us (6%)
  local copies, waits for them, and re-layouts  37.9 us (5%)
  matrix products  32.3 us (5%)
  other arithmetic  27.2 us (4%)
  between operations  13.4 us (2%)
    ppermute x16, waiting for transfers between devices, passed_along(): lax.ppermute(value, axis, [(source, source + steps) for source in range(l...  216 us
    all_gather x1, blocking collectives, local(): lax.all_gather(step_weight, 'seq', axis=0, tiled=True)  160 us
    all_gather x1, waiting for transfers between devices, local(): lax.all_gather(gate_weight, 'seq', axis=0, tiled=True)  93.2 us
    all_to_all x1, waiting for transfers between devices, swapped_in(): return jnp.concatenate(lax.all_to_all(stack, axis, 0, 0), axis=dim)  68.6 us
    ppermute x16, starting transfers between devices, passed_along(): lax.ppermute(value, axis, [(source, source + steps) for source in range(l...  31.8 us
    dot_general x4, matrix products, local(): jnp.dot(gathered, weight_piece, preferred_element_type=jnp.float32)  25.6 us
  transfers between devices with their start and end apart: 20, of which 18 were waited for; matrix products, arithmetic and copies ran while one was open for 4% of the time, Pallas kernels for 0%

profile of v1, /device:TPU:48, one launch (start us, length us, event | category | flops | bytes accessed | tf_op | source)
XLA Modules:
  0.0 699.1 jit_solution(10771718953232695658)
XLA Ops:
  6.5 5.3 stack.2
  11.9 7.1 %all-to-all-start = ((bf16[32,32,4096]{2,1,0:T(8,128)(2,1)}), bf16[32,32,4096]{2,1,0:T(8,128)(2,1)}, u32[]{:S(2)}, u32[]{:S(2)}) async-start(bf16[32,32,4096]{2,1,0:T(8,128)(2,1)} %stack.2), calls=%async_computation | async-start | bytes 16777216 | tf_op jit(solution)/shard_map/all_to_all | solution.py:13
  21.9 159.7 %all_gather.14 = bf16[4096,4]{0,1:T(4,128)(2,1)S(1)} all-gather(bf16[256,4]{0,1:T(4,128)(2,1)S(1)} %copy-done.6), channel_id=1, replica_groups=mesh['seq'=16,'head'=32] {'seq'}, dimensions={0}, use_global_device_ids=true | all-gather | bytes 34816 | tf_op jit(solution)/shard_map/all_gather | solution.py:142
  182.5 68.6 %all-to-all-done = bf16[32,32,4096]{2,1,0:T(8,128)(2,1)} async-done(((bf16[32,32,4096]{2,1,0:T(8,128)(2,1)}), bf16[32,32,4096]{2,1,0:T(8,128)(2,1)}, u32[]{:S(2)}, u32[]{:S(2)}) %all-to-all-start) | async-done | bytes 8388640 | tf_op jit(solution)/shard_map/all_to_all | solution.py:13
  251.1 6.3 fusion.29
  258.2 4.5 all-gather.5.cloned.1.call-done
  262.7 6.3 convolution_convert_fusion.1
  269.9 2.1 collective-permute-start.1
  272.0 93.2 %all-gather.7.cloned.1.call-done = bf16[4096,256]{1,0:T(8,128)(2,1)} async-done(((bf16[256,256]{1,0:T(8,128)(2,1)}), bf16[4096,256]{1,0:T(8,128)(2,1)}) %all-gather.7.cloned.1.call-update) | async-done | bytes 2097168 | tf_op jit(solution)/shard_map/all_gather | solution.py:140
  365.1 7.3 %convert_multiply_fusion = f32[1024,256]{1,0:T(8,128)} fusion(bf16[1024,4096]{1,0:T(8,128)(2,1)} %bitcast.19, bf16[4096,256]{1,0:T(8,128)(2,1)} %all-gather.7.cloned.1.call-done), kind=kOutput, calls=%fused_computation.49 | convolution fusion | flops 2149056512 | bytes 11534336 | tf_op jit(solution)/shard_map/dot_general | solution.py:146
  372.4 5.7 broadcast_multiply_fusion
  378.1 2.1 reshape.264
  381.8 3.6 multiply_convert_fusion.4
  385.4 2.0 reshape.263
  389.1 2.7 multiply_convert_fusion.3
  391.9 36.7 %while.43 = (s32[]{:T(128)}, f32[4,256,256]{1,2,0:T(8,128)}, f32[4,4,128,64]{2,3,1,0:T(8,128)}, f32[4,4]{1,0:T(4,128)S(1)}, f32[4,4,256]{2,1,0:T(4,128)S(1)}, /*...) while((s32[]{:T(128)}, f32[4,256,256]{1,2,0:T(8,128)}, ...), condition=%wide.region_5.6_spmd, body=%wide.region_2.5_spmd.sunk | while | flops 69210640 | bytes 2915319 | solution.py:80
  428.6 7.8 %while.45 = (s32[]{:T(128)}, f32[4,128,64]{2,1,0:T(8,128)S(1)}, f32[4]{0:T(128)S(1)}, f32[4,4,128,64]{3,2,1,0:T(8,128)}, f32[4,4]{1,0:T(4,128)S(1)}, /*index=5*/...) while((s32[]{:T(128)}, f32[4,128,64]{2,1,0:T(8,128)S(1)}, f32[4]{0:T(128)S(1)}, ...), condition=%wide.region_7.8_spmd.clone, body=%wide.region_6.7_spmd.clone.sunk | while | flops 131083 | bytes 1310977 | solution.py:98
  436.4 247.5 %while.44 = (s32[]{:T(128)}, f32[4,128,64]{2,1,0:T(8,128)S(1)}, f32[4]{0:T(128)S(1)}, f32[4,128,64]{2,1,0:T(8,128)S(1)}, s32[]{:T(128)}) while((s32[]{:T(128)}, f32[4,128,64]{2,1,0:T(8,128)S(1)}, f32[4]{0:T(128)S(1)}, f32[4,128,64]{2,1,0:T(8,128)S(1)}, s32[]{:T(128)}) %tuple.85), condition=%wide.region_9.10_spmd, body=%wide.region_8.9_spmd.sunk | while | flops 65538 | bytes 917621 | solution.py:179
  436.6 2.8 collective-permute-start
  439.4 12.6 %collective-permute-done = f32[4,128,64]{2,1,0:T(8,128)S(1)} collective-permute-done((f32[4,128,64]{2,1,0:T(8,128)S(1)}, f32[4,128,64]{2,1,0:T(8,128)S(1)}, u32[]{:S(2)}, u32[]{:S(2)}) %collective-permute-start) | collective-permute-done | bytes 131104 | tf_op jit(solution)/shard_map/while/body/eval_jaxpr/ppermute | solution.py:19
  452.1 1.9 collective-permute-start
  454.0 15.3 %collective-permute-done = f32[4,128,64]{2,1,0:T(8,128)S(1)} collective-permute-done((f32[4,128,64]{2,1,0:T(8,128)S(1)}, f32[4,128,64]{2,1,0:T(8,128)S(1)}, u32[]{:S(2)}, u32[]{:S(2)}) %collective-permute-start) | collective-permute-done | bytes 131104 | tf_op jit(solution)/shard_map/while/body/eval_jaxpr/ppermute | solution.py:19
  469.4 1.9 collective-permute-start
  471.3 15.1 %collective-permute-done = f32[4,128,64]{2,1,0:T(8,128)S(1)} collective-permute-done((f32[4,128,64]{2,1,0:T(8,128)S(1)}, f32[4,128,64]{2,1,0:T(8,128)S(1)}, u32[]{:S(2)}, u32[]{:S(2)}) %collective-permute-start) | collective-permute-done | bytes 131104 | tf_op jit(solution)/shard_map/while/body/eval_jaxpr/ppermute | solution.py:19
  486.5 1.9 collective-permute-start
  488.4 15.1 %collective-permute-done = f32[4,128,64]{2,1,0:T(8,128)S(1)} collective-permute-done((f32[4,128,64]{2,1,0:T(8,128)S(1)}, f32[4,128,64]{2,1,0:T(8,128)S(1)}, u32[]{:S(2)}, u32[]{:S(2)}) %collective-permute-start) | collective-permute-done | bytes 131104 | tf_op jit(solution)/shard_map/while/body/eval_jaxpr/ppermute | solution.py:19
  503.6 1.9 collective-permute-start
  505.5 19.9 %collective-permute-done = f32[4,128,64]{2,1,0:T(8,128)S(1)} collective-permute-done((f32[4,128,64]{2,1,0:T(8,128)S(1)}, f32[4,128,64]{2,1,0:T(8,128)S(1)}, u32[]{:S(2)}, u32[]{:S(2)}) %collective-permute-start) | collective-permute-done | bytes 131104 | tf_op jit(solution)/shard_map/while/body/eval_jaxpr/ppermute | solution.py:19
  525.5 1.9 collective-permute-start
  527.4 17.7 %collective-permute-done = f32[4,128,64]{2,1,0:T(8,128)S(1)} collective-permute-done((f32[4,128,64]{2,1,0:T(8,128)S(1)}, f32[4,128,64]{2,1,0:T(8,128)S(1)}, u32[]{:S(2)}, u32[]{:S(2)}) %collective-permute-start) | collective-permute-done | bytes 131104 | tf_op jit(solution)/shard_map/while/body/eval_jaxpr/ppermute | solution.py:19
  545.2 1.9 collective-permute-start
  547.1 15.2 %collective-permute-done = f32[4,128,64]{2,1,0:T(8,128)S(1)} collective-permute-done((f32[4,128,64]{2,1,0:T(8,128)S(1)}, f32[4,128,64]{2,1,0:T(8,128)S(1)}, u32[]{:S(2)}, u32[]{:S(2)}) %collective-permute-start) | collective-permute-done | bytes 131104 | tf_op jit(solution)/shard_map/while/body/eval_jaxpr/ppermute | solution.py:19
  562.4 1.9 collective-permute-start
  564.3 14.3 %collective-permute-done = f32[4,128,64]{2,1,0:T(8,128)S(1)} collective-permute-done((f32[4,128,64]{2,1,0:T(8,128)S(1)}, f32[4,128,64]{2,1,0:T(8,128)S(1)}, u32[]{:S(2)}, u32[]{:S(2)}) %collective-permute-start) | collective-permute-done | bytes 131104 | tf_op jit(solution)/shard_map/while/body/eval_jaxpr/ppermute | solution.py:19
  578.7 1.9 collective-permute-start
  580.6 16.3 %collective-permute-done = f32[4,128,64]{2,1,0:T(8,128)S(1)} collective-permute-done((f32[4,128,64]{2,1,0:T(8,128)S(1)}, f32[4,128,64]{2,1,0:T(8,128)S(1)}, u32[]{:S(2)}, u32[]{:S(2)}) %collective-permute-start) | collective-permute-done | bytes 131104 | tf_op jit(solution)/shard_map/while/body/eval_jaxpr/ppermute | solution.py:19
  597.0 1.9 collective-permute-start
  598.9 13.1 %collective-permute-done = f32[4,128,64]{2,1,0:T(8,128)S(1)} collective-permute-done((f32[4,128,64]{2,1,0:T(8,128)S(1)}, f32[4,128,64]{2,1,0:T(8,128)S(1)}, u32[]{:S(2)}, u32[]{:S(2)}) %collective-permute-start) | collective-permute-done | bytes 131104 | tf_op jit(solution)/shard_map/while/body/eval_jaxpr/ppermute | solution.py:19
  612.1 1.9 collective-permute-start
  614.1 12.4 %collective-permute-done = f32[4,128,64]{2,1,0:T(8,128)S(1)} collective-permute-done((f32[4,128,64]{2,1,0:T(8,128)S(1)}, f32[4,128,64]{2,1,0:T(8,128)S(1)}, u32[]{:S(2)}, u32[]{:S(2)}) %collective-permute-start) | collective-permute-done | bytes 131104 | tf_op jit(solution)/shard_map/while/body/eval_jaxpr/ppermute | solution.py:19
  628.5 12.4 %collective-permute-done = f32[4,128,64]{2,1,0:T(8,128)S(1)} collective-permute-done((f32[4,128,64]{2,1,0:T(8,128)S(1)}, f32[4,128,64]{2,1,0:T(8,128)S(1)}, u32[]{:S(2)}, u32[]{:S(2)}) %collective-permute-start) | collective-permute-done | bytes 131104 | tf_op jit(solution)/shard_map/while/body/eval_jaxpr/ppermute | solution.py:19
  640.9 1.9 collective-permute-start
  642.8 12.4 %collective-permute-done = f32[4,128,64]{2,1,0:T(8,128)S(1)} collective-permute-done((f32[4,128,64]{2,1,0:T(8,128)S(1)}, f32[4,128,64]{2,1,0:T(8,128)S(1)}, u32[]{:S(2)}, u32[]{:S(2)}) %collective-permute-start) | collective-permute-done | bytes 131104 | tf_op jit(solution)/shard_map/while/body/eval_jaxpr/ppermute | solution.py:19
  655.3 1.9 collective-permute-start
  657.2 12.4 %collective-permute-done = f32[4,128,64]{2,1,0:T(8,128)S(1)} collective-permute-done((f32[4,128,64]{2,1,0:T(8,128)S(1)}, f32[4,128,64]{2,1,0:T(8,128)S(1)}, u32[]{:S(2)}, u32[]{:S(2)}) %collective-permute-start) | collective-permute-done | bytes 131104 | tf_op jit(solution)/shard_map/while/body/eval_jaxpr/ppermute | solution.py:19
  671.6 12.4 %collective-permute-done = f32[4,128,64]{2,1,0:T(8,128)S(1)} collective-permute-done((f32[4,128,64]{2,1,0:T(8,128)S(1)}, f32[4,128,64]{2,1,0:T(8,128)S(1)}, u32[]{:S(2)}, u32[]{:S(2)}) %collective-permute-start) | collective-permute-done | bytes 131104 | tf_op jit(solution)/shard_map/while/body/eval_jaxpr/ppermute | solution.py:19
  684.0 2.3 multiply_add_fusion.1
  688.4 2.0 multiply_convert_fusion.2
  (214 shorter events, 57.1 us)
Async XLA Ops:
  6.5 12.5 %copy-start = (bf16[8,256,256]{2,1,0:T(8,128)(2,1)S(1)}, bf16[8,256,256]{2,1,0:T(8,128)(2,1)}, u32[]{:S(2)}) copy-start(bf16[8,256,256]{2,1,0:T(8,128)(2,1)} %param.20) | copy-start | bytes 3145732
  11.9 9.4 %copy-start.7 = (s32[16]{0:T(128)S(1)}, s32[16]{0:T(128)}, u32[]{:S(2)}) copy-start(s32[16]{0:T(128)} %param.17) | copy-start | bytes 196
  11.9 10.0 %copy-start.6 = (bf16[256,4]{0,1:T(4,128)(2,1)S(1)}, bf16[256,4]{0,1:T(4,128)(2,1)}, u32[]{:S(2)}) copy-start(bf16[256,4]{0,1:T(4,128)(2,1)} %param.21) | copy-start | bytes 6148
  11.9 170.5 %copy-start.8 = (f32[4]{0:T(128)S(1)}, f32[4]{0:T(128)}, u32[]{:S(2)}) copy-start(f32[4]{0:T(128)} %param.25) | copy-start | bytes 52
  11.9 170.6 %copy-start.5 = (f32[4,256]{1,0:T(4,128)S(1)}, f32[4,256]{1,0:T(4,128)}, u32[]{:S(2)}) copy-start(f32[4,256]{1,0:T(4,128)} %param.22) | copy-start | bytes 12292
  11.9 239.2 %all-to-all-start = ((bf16[32,32,4096]{2,1,0:T(8,128)(2,1)}), bf16[32,32,4096]{2,1,0:T(8,128)(2,1)}, u32[]{:S(2)}, u32[]{:S(2)}) async-start(bf16[32,32,4096]{2,1,0:T(8,128)(2,1)} %stack.2), calls=%async_computation | async-start | bytes 16777216 | tf_op jit(solution)/shard_map/all_to_all | solution.py:13
  19.0 163.5 %all-gather.9.cloned.1.call-start = ((), (), s32[]{:S(2)}) async-start(), calls=%async_computation.3 | async-start | bytes 2228224 | tf_op jit(solution)/shard_map/all_gather | solution.py:141
  19.8 242.9 %all-gather.5.cloned.1.call-start = ((), (), s32[]{:S(2)}) async-start(), calls=%async_computation.1 | async-start | bytes 2228224 | tf_op jit(solution)/shard_map/all_gather | solution.py:139
  20.5 344.6 %all-gather.7.cloned.1.call-start = ((), (), s32[]{:S(2)}) async-start(), calls=%async_computation.2 | async-start | bytes 2228224 | tf_op jit(solution)/shard_map/all_gather | solution.py:140
  257.4 0.8 copy-start.2
  269.0 0.8 copy-start.3
  269.8 102.6 %copy-start.4 = (f32[4]{0:T(128)S(1)}, f32[4]{0:T(128)}, u32[]{:S(2)}) copy-start(f32[4]{0:T(128)} %param.24) | copy-start | bytes 52
  269.9 112.0 %collective-permute-start.1 = (bf16[3,512]{1,0:T(4,128)(2,1)S(1)}, bf16[3,512]{1,0:T(4,128)(2,1)S(1)}, u32[]{:S(2)}, u32[]{:S(2)}) collective-permute-start(bf16[3,512]{1,0:T(4,128)(2,1)S(1)} %pad_maximum_fusion.2), channel_id=1, source_target_pairs={{0,32},{32,64},{64,96},{96,128},{128,160},{160,192},{192,224},{224... | collective-permute-start | bytes 9224 | tf_op jit(solution)/shard_map/ppermute | solution.py:19
  428.6 259.8 %copy-start.1 = (f32[4,256,4,64]{1,3,2,0:T(8,128)S(1)}, f32[4,256,4,64]{1,3,2,0:T(8,128)}, u32[]{:S(2)}) copy-start(f32[4,256,4,64]{1,3,2,0:T(8,128)} %copy.55) | copy-start | bytes 3145732
  436.6 15.4 %collective-permute-start = (f32[4,128,64]{2,1,0:T(8,128)S(1)}, f32[4,128,64]{2,1,0:T(8,128)S(1)}, u32[]{:S(2)}, u32[]{:S(2)}) collective-permute-start(f32[4,128,64]{2,1,0:T(8,128)S(1)} %multiply_add_fusion.3), channel_id=1, source_target_pairs={{0,32},{32,64},{64,96},{96,128},{128,160},{160,192},{192,224},{224... | collective-permute-start | bytes 393224 | tf_op jit(solution)/shard_map/while/body/eval_jaxpr/ppermute | solution.py:19
  452.1 17.2 %collective-permute-start = (f32[4,128,64]{2,1,0:T(8,128)S(1)}, f32[4,128,64]{2,1,0:T(8,128)S(1)}, u32[]{:S(2)}, u32[]{:S(2)}) collective-permute-start(f32[4,128,64]{2,1,0:T(8,128)S(1)} %multiply_add_fusion.3), channel_id=1, source_target_pairs={{0,32},{32,64},{64,96},{96,128},{128,160},{160,192},{192,224},{224... | collective-permute-start | bytes 393224 | tf_op jit(solution)/shard_map/while/body/eval_jaxpr/ppermute | solution.py:19
  469.4 17.0 %collective-permute-start = (f32[4,128,64]{2,1,0:T(8,128)S(1)}, f32[4,128,64]{2,1,0:T(8,128)S(1)}, u32[]{:S(2)}, u32[]{:S(2)}) collective-permute-start(f32[4,128,64]{2,1,0:T(8,128)S(1)} %multiply_add_fusion.3), channel_id=1, source_target_pairs={{0,32},{32,64},{64,96},{96,128},{128,160},{160,192},{192,224},{224... | collective-permute-start | bytes 393224 | tf_op jit(solution)/shard_map/while/body/eval_jaxpr/ppermute | solution.py:19
  486.5 17.0 %collective-permute-start = (f32[4,128,64]{2,1,0:T(8,128)S(1)}, f32[4,128,64]{2,1,0:T(8,128)S(1)}, u32[]{:S(2)}, u32[]{:S(2)}) collective-permute-start(f32[4,128,64]{2,1,0:T(8,128)S(1)} %multiply_add_fusion.3), channel_id=1, source_target_pairs={{0,32},{32,64},{64,96},{96,128},{128,160},{160,192},{192,224},{224... | collective-permute-start | bytes 393224 | tf_op jit(solution)/shard_map/while/body/eval_jaxpr/ppermute | solution.py:19
  503.6 21.8 %collective-permute-start = (f32[4,128,64]{2,1,0:T(8,128)S(1)}, f32[4,128,64]{2,1,0:T(8,128)S(1)}, u32[]{:S(2)}, u32[]{:S(2)}) collective-permute-start(f32[4,128,64]{2,1,0:T(8,128)S(1)} %multiply_add_fusion.3), channel_id=1, source_target_pairs={{0,32},{32,64},{64,96},{96,128},{128,160},{160,192},{192,224},{224... | collective-permute-start | bytes 393224 | tf_op jit(solution)/shard_map/while/body/eval_jaxpr/ppermute | solution.py:19
  525.5 19.6 %collective-permute-start = (f32[4,128,64]{2,1,0:T(8,128)S(1)}, f32[4,128,64]{2,1,0:T(8,128)S(1)}, u32[]{:S(2)}, u32[]{:S(2)}) collective-permute-start(f32[4,128,64]{2,1,0:T(8,128)S(1)} %multiply_add_fusion.3), channel_id=1, source_target_pairs={{0,32},{32,64},{64,96},{96,128},{128,160},{160,192},{192,224},{224... | collective-permute-start | bytes 393224 | tf_op jit(solution)/shard_map/while/body/eval_jaxpr/ppermute | solution.py:19
  545.2 17.1 %collective-permute-start = (f32[4,128,64]{2,1,0:T(8,128)S(1)}, f32[4,128,64]{2,1,0:T(8,128)S(1)}, u32[]{:S(2)}, u32[]{:S(2)}) collective-permute-start(f32[4,128,64]{2,1,0:T(8,128)S(1)} %multiply_add_fusion.3), channel_id=1, source_target_pairs={{0,32},{32,64},{64,96},{96,128},{128,160},{160,192},{192,224},{224... | collective-permute-start | bytes 393224 | tf_op jit(solution)/shard_map/while/body/eval_jaxpr/ppermute | solution.py:19
  562.4 16.2 %collective-permute-start = (f32[4,128,64]{2,1,0:T(8,128)S(1)}, f32[4,128,64]{2,1,0:T(8,128)S(1)}, u32[]{:S(2)}, u32[]{:S(2)}) collective-permute-start(f32[4,128,64]{2,1,0:T(8,128)S(1)} %multiply_add_fusion.3), channel_id=1, source_target_pairs={{0,32},{32,64},{64,96},{96,128},{128,160},{160,192},{192,224},{224... | collective-permute-start | bytes 393224 | tf_op jit(solution)/shard_map/while/body/eval_jaxpr/ppermute | solution.py:19
  578.7 18.2 %collective-permute-start = (f32[4,128,64]{2,1,0:T(8,128)S(1)}, f32[4,128,64]{2,1,0:T(8,128)S(1)}, u32[]{:S(2)}, u32[]{:S(2)}) collective-permute-start(f32[4,128,64]{2,1,0:T(8,128)S(1)} %multiply_add_fusion.3), channel_id=1, source_target_pairs={{0,32},{32,64},{64,96},{96,128},{128,160},{160,192},{192,224},{224... | collective-permute-start | bytes 393224 | tf_op jit(solution)/shard_map/while/body/eval_jaxpr/ppermute | solution.py:19
  597.0 15.0 %collective-permute-start = (f32[4,128,64]{2,1,0:T(8,128)S(1)}, f32[4,128,64]{2,1,0:T(8,128)S(1)}, u32[]{:S(2)}, u32[]{:S(2)}) collective-permute-start(f32[4,128,64]{2,1,0:T(8,128)S(1)} %multiply_add_fusion.3), channel_id=1, source_target_pairs={{0,32},{32,64},{64,96},{96,128},{128,160},{160,192},{192,224},{224... | collective-permute-start | bytes 393224 | tf_op jit(solution)/shard_map/while/body/eval_jaxpr/ppermute | solution.py:19
  612.1 14.3 %collective-permute-start = (f32[4,128,64]{2,1,0:T(8,128)S(1)}, f32[4,128,64]{2,1,0:T(8,128)S(1)}, u32[]{:S(2)}, u32[]{:S(2)}) collective-permute-start(f32[4,128,64]{2,1,0:T(8,128)S(1)} %multiply_add_fusion.3), channel_id=1, source_target_pairs={{0,32},{32,64},{64,96},{96,128},{128,160},{160,192},{192,224},{224... | collective-permute-start | bytes 393224 | tf_op jit(solution)/shard_map/while/body/eval_jaxpr/ppermute | solution.py:19
  626.5 14.3 %collective-permute-start = (f32[4,128,64]{2,1,0:T(8,128)S(1)}, f32[4,128,64]{2,1,0:T(8,128)S(1)}, u32[]{:S(2)}, u32[]{:S(2)}) collective-permute-start(f32[4,128,64]{2,1,0:T(8,128)S(1)} %multiply_add_fusion.3), channel_id=1, source_target_pairs={{0,32},{32,64},{64,96},{96,128},{128,160},{160,192},{192,224},{224... | collective-permute-start | bytes 393224 | tf_op jit(solution)/shard_map/while/body/eval_jaxpr/ppermute | solution.py:19
  640.9 14.3 %collective-permute-start = (f32[4,128,64]{2,1,0:T(8,128)S(1)}, f32[4,128,64]{2,1,0:T(8,128)S(1)}, u32[]{:S(2)}, u32[]{:S(2)}) collective-permute-start(f32[4,128,64]{2,1,0:T(8,128)S(1)} %multiply_add_fusion.3), channel_id=1, source_target_pairs={{0,32},{32,64},{64,96},{96,128},{128,160},{160,192},{192,224},{224... | collective-permute-start | bytes 393224 | tf_op jit(solution)/shard_map/while/body/eval_jaxpr/ppermute | solution.py:19
  655.3 14.3 %collective-permute-start = (f32[4,128,64]{2,1,0:T(8,128)S(1)}, f32[4,128,64]{2,1,0:T(8,128)S(1)}, u32[]{:S(2)}, u32[]{:S(2)}) collective-permute-start(f32[4,128,64]{2,1,0:T(8,128)S(1)} %multiply_add_fusion.3), channel_id=1, source_target_pairs={{0,32},{32,64},{64,96},{96,128},{128,160},{160,192},{192,224},{224... | collective-permute-start | bytes 393224 | tf_op jit(solution)/shard_map/while/body/eval_jaxpr/ppermute | solution.py:19
  669.7 14.3 %collective-permute-start = (f32[4,128,64]{2,1,0:T(8,128)S(1)}, f32[4,128,64]{2,1,0:T(8,128)S(1)}, u32[]{:S(2)}, u32[]{:S(2)}) collective-permute-start(f32[4,128,64]{2,1,0:T(8,128)S(1)} %multiply_add_fusion.3), channel_id=1, source_target_pairs={{0,32},{32,64},{64,96},{96,128},{128,160},{160,192},{192,224},{224... | collective-permute-start | bytes 393224 | tf_op jit(solution)/shard_map/while/body/eval_jaxpr/ppermute | solution.py:19
Sparse Core Ops, SparseCore 0:
  23.0 129.9 all-gather.8
  156.2 106.4 all-gather.4
  265.9 99.1 all-gather.6
